TPU v7x, 32 devices: a whole 2x2x4 slice. The times are simulated.
32 devices in a mesh: snap: 8 (over z, x), feat: 4 (over y, core).
Axes of the slice: x: 2, y: 2, z: 4, core: 2. Of those that a mesh axis runs over, the one named last changes fastest.
Arguments:
- node_features: bfloat16 [16, 512, 256], P('snap', None, 'feat'), may hold values from -6 to 6
- tile_rows: int32 [16, 8], P('snap'), may hold values from 0 to 3
- tile_cols: int32 [16, 8], P('snap'), may hold values from 0 to 3, as said below
- tile_counts: int32 [16], P('snap'), may hold values from 4 to 8, as said below
- tile_values: bfloat16 [16, 8, 128, 128], P('snap'), may hold values from -0.5 to 0.5
- layer_one: bfloat16 [256, 256], replicated, may hold values from -0.375 to 0.375
- layer_two: bfloat16 [256, 256], replicated, may hold values from -0.375 to 0.375
- query_weight: bfloat16 [256, 256], replicated, may hold values from -1.25 to 1.25
- key_weight: bfloat16 [256, 256], replicated, may hold values from -1.25 to 1.25
- value_weight: bfloat16 [256, 256], replicated, may hold values from -0.375 to 0.375
- out_weight: bfloat16 [256, 256], replicated, may hold values from -0.375 to 0.375
Outputs:
- evolved: bfloat16 [16, 512, 256], P('snap', None, 'feat')
Inputs may be any that keep to these rules, and one draw needn't show every extreme that they name: `tile_cols`: block columns of the tile slots; a coordinate pair may be listed more than once, and such tiles add. `tile_counts`: some snapshot uses all 8 slots.
All inputs are finite; a program needn't handle non-finite values.
Results may differ from a plain program's by a relative error of at most 0.02.
The roundings to bfloat16 on the way count: a program that leaves them out, or rounds other values in their place, can miss the bound.
Values may be sent and summed in bfloat16 or wider, within the bound.
A program may use at most 64 MiB of HBM per device.

v0:
```python
import jax
import jax.numpy as jnp
from jax import lax
from jax.sharding import PartitionSpec as P

HEADS = 8


masked_score = -1e30


def spread_padded(features, tile_block, block_rows, block_cols, slot_count):
    vert_count, feat_width = features.shape
    tile_side = tile_block.shape[1]
    slot_total = tile_block.shape[0]
    block_count = vert_count // tile_side
    blocked = features.reshape(block_count, tile_side, feat_width)
    picked_blocks = blocked[block_cols]
    live_slots = jnp.arange(slot_total, dtype=jnp.int32) < slot_count
    products = jnp.einsum(
        "irc,icf->irf", tile_block, picked_blocks, preferred_element_type=jnp.float32
    )
    products = products * live_slots.astype(jnp.float32)[:, None, None]
    membership = (
        (block_rows[None, :] == jnp.arange(block_count, dtype=jnp.int32)[:, None])
        & live_slots[None, :]
    ).astype(jnp.float32)
    summed = jnp.dot(
        membership,
        products.reshape(slot_total, tile_side * feat_width),
        precision=lax.Precision.HIGHEST,
    )
    return summed.reshape(vert_count, feat_width).astype(jnp.bfloat16)


def attend_local(hidden, query_weight, key_weight, value_weight, out_weight):
    snaps, verts, model_width = hidden.shape
    head_dim = model_width // HEADS
    flat = hidden.reshape(snaps * verts, model_width)

    def project(weight):
        return (
            jnp.dot(flat, weight, preferred_element_type=jnp.float32)
            .astype(jnp.bfloat16)
            .reshape(snaps, verts, HEADS, head_dim)
        )

    query_heads = project(query_weight)
    key_heads = project(key_weight)
    value_heads = project(value_weight)
    scores = jnp.einsum(
        "tvhd,uvhd->vhtu", query_heads, key_heads, preferred_element_type=jnp.float32
    ) * head_dim ** (-0.5)
    causal = (
        jnp.arange(snaps, dtype=jnp.int32)[:, None] >= jnp.arange(snaps, dtype=jnp.int32)[None, :]
    )
    scores = jnp.where(causal, scores, masked_score)
    row_max = jnp.max(scores, axis=-1, keepdims=True)
    lifted = jnp.exp(scores - row_max)
    weights = (lifted / jnp.sum(lifted, axis=-1, keepdims=True)).astype(jnp.bfloat16)
    context = jnp.einsum(
        "vhtu,uvhd->tvhd", weights, value_heads, preferred_element_type=jnp.float32
    ).astype(jnp.bfloat16)
    context = context.reshape(snaps * verts, model_width)
    result = flat.astype(jnp.float32) + jnp.dot(
        context, out_weight, preferred_element_type=jnp.float32
    )
    return result.astype(jnp.bfloat16).reshape(snaps, verts, model_width)


def on_device(
    node_features,
    tile_rows,
    tile_cols,
    tile_counts,
    tile_values,
    layer_one,
    layer_two,
    query_weight,
    key_weight,
    value_weight,
    out_weight,
):
    snap_dev, vert_count, feat_width = node_features.shape
    feat_index = lax.axis_index("feat")

    def spread_all(features):
        spread_pieces = []
        for snapshot in range(snap_dev):
            spread_pieces.append(
                spread_padded(
                    features[snapshot],
                    tile_values[snapshot],
                    tile_rows[snapshot],
                    tile_cols[snapshot],
                    tile_counts[snapshot],
                )
            )
        return jnp.stack(spread_pieces, axis=0)

    def convolve(features, weight):
        spread_rows = spread_all(features).reshape(snap_dev * vert_count, feat_width)
        own_columns = lax.dynamic_slice_in_dim(weight, feat_index * feat_width, feat_width, 1)
        mixed_sum = jnp.dot(
            lax.all_gather(spread_rows, "feat", axis=1, tiled=True),
            own_columns,
            preferred_element_type=jnp.float32,
        )
        mixed_sum = mixed_sum.reshape(snap_dev, vert_count, feat_width)
        return (features.astype(jnp.float32) + jnp.maximum(mixed_sum, 0.0)).astype(jnp.bfloat16)

    hidden_one = convolve(node_features, layer_one)
    hidden_two = convolve(hidden_one, layer_two)
    vertex_rows = lax.all_to_all(
        lax.all_to_all(hidden_two, "snap", split_axis=1, concat_axis=0, tiled=True),
        "feat",
        split_axis=1,
        concat_axis=2,
        tiled=True,
    )
    attended = attend_local(vertex_rows, query_weight, key_weight, value_weight, out_weight)
    return lax.all_to_all(
        lax.all_to_all(attended, "feat", split_axis=2, concat_axis=1, tiled=True),
        "snap",
        split_axis=0,
        concat_axis=1,
        tiled=True,
    )


def solution(mesh):
    placed = (
        P("snap", None, "feat"),
        P("snap", None),
        P("snap", None),
        P("snap"),
        P("snap", None, None, None),
        P(),
        P(),
        P(),
        P(),
        P(),
        P(),
    )
    return jax.shard_map(
        on_device, mesh=mesh, in_specs=placed, out_specs=P("snap", None, "feat"), check_vma=False
    )
```

profile of v0, /device:TPU:0, one launch (start us, length us, event | category | flops | bytes accessed | tf_op | source)
XLA Modules:
  0.0 81.3 jit_solution(12368943352257759503)
XLA Ops:
  0.0 0.7 copy-done.9
  0.7 0.9 %fusion.47 = (bf16[1,512,64]{1,2,0:T(8,128)(2,1)S(1)}, bf16[1,512,64]{1,2,0:T(8,128)(2,1)S(1)}) fusion(bf16[2,512,64]{1,2,0:T(8,128)(2,1)} %param.11), kind=kLoop, calls=%fused_computation.79 | loop fusion | bytes 262144 | tf_op jit(solution)/shard_map/slice | solution.py:92
  1.7 0.6 copy-done.8
  2.4 0.6 fusion.48
  3.0 0.6 iota_compare_fusion.4
  3.6 0.6 gather_fusion
  4.2 0.3 fusion.8
  4.5 0.2 copy.104
  4.7 0.2 reshape.167
  4.9 0.5 copy-done.10
  5.4 0.2 convolution_convert_fusion.3
  5.9 0.6 iota_compare_fusion.3
  6.5 0.6 gather_fusion.1
  7.1 0.3 fusion.7
  7.4 0.2 copy.106
  7.6 0.2 reshape.168
  7.8 0.2 convolution_convert_fusion.2
  8.4 8.7 %all_gather.6 = bf16[1024,256]{0,1:T(8,128)(2,1)S(1)} all-gather(bf16[1024,64]{0,1:T(8,128)(2,1)S(1)} %copy.107), channel_id=1, replica_groups=mesh['snap'=8,'feat'=4] {'feat'}, dimensions={1}, use_global_device_ids=true | all-gather | bytes 655360 | tf_op jit(solution)/shard_map/all_gather | solution.py:105
  17.1 0.3 convolution_maximum_fusion.1
  17.4 0.6 copy-done.2
  18.1 0.6 gather_fusion.2
  18.6 0.3 fusion.6
  18.9 0.2 copy.110
  19.1 0.2 reshape.170
  19.3 0.2 convolution_convert_fusion.1
  19.8 0.6 gather_fusion.3
  20.4 0.3 fusion.5
  20.6 0.2 copy.112
  20.9 0.2 reshape.171
  21.0 0.2 convolution_convert_fusion
  21.7 7.4 %all_gather.7 = bf16[1024,256]{0,1:T(8,128)(2,1)S(1)} all-gather(bf16[1024,64]{0,1:T(8,128)(2,1)S(1)} %copy.113), channel_id=1, replica_groups=mesh['snap'=8,'feat'=4] {'feat'}, dimensions={1}, use_global_device_ids=true | all-gather | bytes 655360 | tf_op jit(solution)/shard_map/all_gather | solution.py:105
  29.1 0.3 convolution_maximum_fusion
  29.6 0.2 reshape.211
  29.9 13.1 %all_to_all.69 = bf16[8,2,4096]{2,1,0:T(2,128)(2,1)S(1)} all-to-all(bf16[8,2,4096]{2,1,0:T(2,128)(2,1)S(1)} %reshape.211), channel_id=1, replica_groups=mesh['snap'=8,'feat'=4] {'snap'}, dimensions={0} | all-to-all | bytes 262144 | tf_op jit(solution)/shard_map/all_to_all | solution.py:115
  43.0 0.2 reshape.212
  43.4 0.9 %reshape.213 = bf16[4,2,8192]{2,1,0:T(2,128)(2,1)} reshape(bf16[64,16,64]{2,1,0:T(8,128)(2,1)S(1)} %bitcast.111) | data formatting | bytes 262144
  44.3 3.3 %all-to-all-start.1 = ((bf16[4,2,8192]{2,1,0:T(2,128)(2,1)}), bf16[4,2,8192]{2,1,0:T(2,128)(2,1)S(1)}, u32[]{:S(2)}, u32[]{:S(2)}) async-start(bf16[4,2,8192]{2,1,0:T(2,128)(2,1)} %reshape.213), calls=%async_computation.1 | async-start | bytes 262144 | tf_op jit(solution)/shard_map/all_to_all | solution.py:114
  47.7 4.6 %all-to-all-done.1 = bf16[4,2,8192]{2,1,0:T(2,128)(2,1)S(1)} async-done(((bf16[4,2,8192]{2,1,0:T(2,128)(2,1)}), bf16[4,2,8192]{2,1,0:T(2,128)(2,1)S(1)}, u32[]{:S(2)}, u32[]{:S(2)}) %all-to-all-start.1) | async-done | bytes 131104 | tf_op jit(solution)/shard_map/all_to_all | solution.py:114
  52.2 0.2 reshape.214
  52.4 0.2 copy.120
  52.7 0.2 reshape.173
  52.9 0.7 copy-done.3
  53.6 0.2 convolution_convert_fusion.6
  53.8 0.2 reshape.175
  54.0 0.7 copy-done.4
  54.7 0.2 convolution_convert_fusion.5
  54.9 0.2 reshape.176
  55.1 0.7 copy-done.5
  55.9 0.2 reshape.174
  56.2 1.0 %fusion.49 = (f32[16,8,16]{2,1,0:T(8,128)S(1)}, f32[16,8,16,16]{2,3,1,0:T(8,128)S(1)}) fusion(bf16[16,16,8,32]{3,2,1,0:T(8,128)(2,1)S(1)} %reshape.176, bf16[16,16,8,32]{3,2,1,0:T(8,128)(2,1)S(1)} %reshape.175, pred[16,16]{0,1:T(8,128)(4,1)S(1)} %iota_compare_fusion), kind=kOutput, calls=%fused_computation.81 | convolution fusion | flops 2228239 | bytes 401664 | tf_op jit(solution)/shard_map/sub | solution.py:59
  57.2 0.5 fusion.4
  57.9 0.4 reshape.177
  58.3 0.5 copy-done.6
  58.8 0.2 fusion.9
  59.0 0.9 %copy.126 = bf16[16,16,256]{1,0,2:T(8,128)(2,1)S(1)} copy(bf16[16,16,256]{2,1,0:T(8,128)(2,1)S(1)} %bitcast.115) | data formatting | bytes 262144 | tf_op jit(solution)/shard_map/reshape | solution.py:68
  60.0 1.1 %reshape.215 = bf16[4,2,8192]{2,1,0:T(2,128)(2,1)S(1)} reshape(bf16[256,16,16]{2,1,0:T(8,128)(2,1)S(1)} %bitcast.102) | data formatting | bytes 262144
  61.0 7.0 %all_to_all.70 = bf16[4,2,8192]{2,1,0:T(2,128)(2,1)S(1)} all-to-all(bf16[4,2,8192]{2,1,0:T(2,128)(2,1)S(1)} %reshape.215), channel_id=1, replica_groups=mesh['snap'=8,'feat'=4] {'feat'}, dimensions={0} | all-to-all | bytes 262144 | tf_op jit(solution)/shard_map/all_to_all | solution.py:123
  68.0 0.7 reshape.216
  68.7 1.2 %copy.134 = bf16[16,16,4,64]{3,2,1,0:T(4,128)(2,1)S(1)} copy(bf16[16,16,4,64]{1,0,3,2:T(8,128)(2,1)S(1)} %bitcast.101) | data formatting | bytes 262144 | tf_op jit(solution)/shard_map/all_to_all | solution.py:123
  69.9 0.2 reshape.217
  70.2 9.9 %all_to_all.71 = bf16[8,2,4096]{2,1,0:T(2,128)(2,1)S(1)} all-to-all(bf16[8,2,4096]{2,1,0:T(2,128)(2,1)S(1)} %reshape.217), channel_id=1, replica_groups=mesh['snap'=8,'feat'=4] {'snap'}, dimensions={0} | all-to-all | bytes 262144 | tf_op jit(solution)/shard_map/all_to_all | solution.py:122
  80.0 0.2 reshape.218
  80.3 0.2 copy.129
  80.5 0.9 %all_to_all.64 = bf16[2,512,64]{1,2,0:T(8,128)(2,1)} reshape(bf16[2,8,64,64]{2,1,3,0:T(8,128)(2,1)S(1)} %copy.129) | data formatting | bytes 262144 | tf_op jit(solution)/shard_map/all_to_all | solution.py:122
  (43 shorter events, 2.0 us)
Async XLA Ops:
  0.0 17.1 %copy-start = (bf16[256,256]{1,0:T(8,128)(2,1)S(1)}, bf16[256,256]{1,0:T(8,128)(2,1)}, u32[]{:S(2)}) copy-start(bf16[256,256]{1,0:T(8,128)(2,1)} %param.16) | copy-start | bytes 393220
  0.0 0.7 copy-start.9
  0.7 3.5 %copy-start.1 = (bf16[2,8,128,128]{3,2,1,0:T(8,128)(2,1)S(1)}, bf16[2,8,128,128]{3,2,1,0:T(8,128)(2,1)}, u32[]{:S(2)}) copy-start(bf16[2,8,128,128]{3,2,1,0:T(8,128)(2,1)} %param.15) | copy-start | bytes 1572868
  1.7 0.7 copy-start.8
  4.7 0.7 copy-start.10
  17.1 0.9 %copy-start.2 = (bf16[2,512,64]{1,2,0:T(8,128)(2,1)S(1)}, bf16[2,512,64]{1,2,0:T(8,128)(2,1)}, u32[]{:S(2)}) copy-start(bf16[2,512,64]{1,2,0:T(8,128)(2,1)} %param.11) | copy-start | bytes 393220
  21.7 7.4 %copy-start.7 = (bf16[256,256]{1,0:T(8,128)(2,1)S(1)}, bf16[256,256]{1,0:T(8,128)(2,1)}, u32[]{:S(2)}) copy-start(bf16[256,256]{1,0:T(8,128)(2,1)} %param.17) | copy-start | bytes 393220
  44.3 7.9 %all-to-all-start.1 = ((bf16[4,2,8192]{2,1,0:T(2,128)(2,1)}), bf16[4,2,8192]{2,1,0:T(2,128)(2,1)S(1)}, u32[]{:S(2)}, u32[]{:S(2)}) async-start(bf16[4,2,8192]{2,1,0:T(2,128)(2,1)} %reshape.213), calls=%async_computation.1 | async-start | bytes 262144 | tf_op jit(solution)/shard_map/all_to_all | solution.py:114
  52.7 0.9 %copy-start.3 = (bf16[256,256]{1,0:T(8,128)(2,1)S(1)}, bf16[256,256]{1,0:T(8,128)(2,1)}, u32[]{:S(2)}) copy-start(bf16[256,256]{1,0:T(8,128)(2,1)} %param.18) | copy-start | bytes 393220
  53.8 0.9 %copy-start.4 = (bf16[256,256]{1,0:T(8,128)(2,1)S(1)}, bf16[256,256]{1,0:T(8,128)(2,1)}, u32[]{:S(2)}) copy-start(bf16[256,256]{1,0:T(8,128)(2,1)} %param.19) | copy-start | bytes 393220
  54.9 0.9 %copy-start.5 = (bf16[256,256]{1,0:T(8,128)(2,1)S(1)}, bf16[256,256]{1,0:T(8,128)(2,1)}, u32[]{:S(2)}) copy-start(bf16[256,256]{1,0:T(8,128)(2,1)} %param.20) | copy-start | bytes 393220
  57.9 0.9 %copy-start.6 = (bf16[256,256]{1,0:T(8,128)(2,1)S(1)}, bf16[256,256]{1,0:T(8,128)(2,1)}, u32[]{:S(2)}) copy-start(bf16[256,256]{1,0:T(8,128)(2,1)} %param.21) | copy-start | bytes 393220
where the time goes:
time: 81.8 us; the launch traced here: 81.3 us
  blocking collectives  46 us (56%)
  local copies, waits for them, and re-layouts  20.4 us (25%)
  matrix products  4.96 us (6%)
  waiting for transfers between devices  4.55 us (6%)
  starting transfers between devices  3.33 us (4%)
  other arithmetic  1.48 us (2%)
    all_gather x2, blocking collectives, convolve(): lax.all_gather(spread_rows, 'feat', axis=1, tiled=True)  16.1 us
    all_to_all x1, blocking collectives, on_device(): lax.all_to_all(hidden_two, 'snap', split_axis=1, concat_axis=0, tiled=True)  13.1 us
    all_to_all x1, blocking collectives, on_device(): lax.all_to_all(lax.all_to_all(attended, 'feat', split_axis=2, concat_axis...  9.86 us
    unnamed x30, local copies, waits for them, and re-layouts  8.75 us
    all_to_all x1, blocking collectives, on_device(): lax.all_to_all(attended, 'feat', split_axis=2, concat_axis=1, tiled=True)  6.99 us
    all_to_all x1, waiting for transfers between devices, on_device(): lax.all_to_all(lax.all_to_all(hidden_two, 'snap', split_axis=1, concat_ax...  4.55 us
    all_to_all x1, starting transfers between devices, on_device(): lax.all_to_all(lax.all_to_all(hidden_two, 'snap', split_axis=1, concat_ax...  3.33 us
    gather x4, local copies, waits for them, and re-layouts, spread_padded(): picked_blocks = blocked[block_cols]  2.29 us
  transfers between devices with their start and end apart: 1, of which 1 were waited for; matrix products, arithmetic and copies ran while one was open for 0% of the time, Pallas kernels for 0%

commit v1 on v0

--- a/solution.py
+++ b/solution.py
@@ -1,6 +1,11 @@
+import functools
+import math
+
 import jax
 import jax.numpy as jnp
 from jax import lax
+from jax.experimental import pallas as pl
+from jax.experimental.pallas import tpu as pltpu
 from jax.sharding import PartitionSpec as P
 
 HEADS = 8
@@ -128,6 +133,310 @@
     )
 
 
+LANES = 128
+SUBLANES = 8
+MESH = pl.DeviceIdType.MESH
+
+
+def fused_kernel(
+    n_snap,
+    n_feat,
+    rows_ref,
+    cols_ref,
+    counts_ref,
+    feat_ref,
+    tiles_ref,
+    w_one,
+    w_two,
+    w_query,
+    w_key,
+    w_value,
+    w_out,
+    out_ref,
+    tiles,
+    weights,
+    pieces,
+    adjacency,
+    features,
+    hidden_one,
+    hidden_two,
+    vertex_rows,
+    outgoing,
+    returned,
+    load_sem,
+    gather_send,
+    gather_recv,
+    spread_send,
+    spread_recv,
+    return_send,
+    return_recv,
+):
+    snap_dev, feat_width, vert_count = feat_ref.shape
+    slot_total, tile_side, _ = tiles.shape
+    block_count = vert_count // tile_side
+    snaps, vert_dev, width = vertex_rows.shape
+    parts = n_feat // snap_dev
+    part_rows = vert_count // parts
+    total = n_snap * n_feat
+    head_dim = width // HEADS
+
+    me_snap = lax.axis_index("snap")
+    me_feat = lax.axis_index("feat")
+    me = me_snap * n_feat + me_feat
+    part = me_feat % parts
+    local = me_feat // parts
+    own = me_snap * snap_dev + local
+
+    def load(source, target, at):
+        copy = pltpu.make_async_copy(source, target, load_sem.at[at])
+        copy.start()
+        return copy
+
+    tile_load = load(tiles_ref.at[local], tiles, 1)
+    weight_loads = [
+        load(ref, weights.at[at], 2 + at)
+        for at, ref in enumerate((w_one, w_two, w_query, w_key, w_value, w_out))
+    ]
+
+    barrier = pltpu.get_barrier_semaphore()
+    for step in range(1, total):
+        peer = (me + step) % total
+        pl.semaphore_signal(
+            barrier, inc=1, device_id=(peer // n_feat, peer % n_feat), device_id_type=MESH
+        )
+
+    pl.semaphore_wait(barrier, total - 1)
+
+    gathers = []
+    for step in [n_feat // 2] + [s for s in range(1, n_feat) if s != n_feat // 2]:
+        peer = (me_feat + step) % n_feat
+        copy = pltpu.make_async_remote_copy(
+            src_ref=feat_ref.at[peer // parts],
+            dst_ref=pieces.at[me_feat],
+            send_sem=gather_send.at[step],
+            recv_sem=gather_recv.at[step],
+            device_id=(me_snap, peer),
+            device_id_type=MESH,
+        )
+        copy.start()
+        gathers.append(copy)
+    own_load = load(feat_ref.at[local], pieces.at[me_feat], 0)
+
+    tile_load.wait()
+    slot_count = counts_ref[local]
+    strip = 2 * SUBLANES
+    places = []
+    for slot in range(slot_total):
+        place = rows_ref[local, slot] * block_count + cols_ref[local, slot]
+        place = jnp.where(slot < slot_count, place, -1)
+        places.append(jnp.full((strip, tile_side), place, jnp.int32))
+
+    def build(at, carry):
+        first = pl.multiple_of(at * strip, strip)
+        listed = [
+            tiles[slot, pl.ds(first, strip), :].astype(jnp.float32) for slot in range(slot_total)
+        ]
+        for row in range(block_count):
+            for col in range(block_count):
+                summed = jnp.zeros((strip, tile_side), jnp.float32)
+                for slot in range(slot_total):
+                    summed += jnp.where(
+                        places[slot] == row * block_count + col, listed[slot], 0.0
+                    )
+                start = pl.multiple_of(row * tile_side + first, strip)
+                adjacency[pl.ds(start, strip), col * tile_side : (col + 1) * tile_side] = (
+                    summed.astype(jnp.bfloat16)
+                )
+        return carry
+
+    lax.fori_loop(0, tile_side // strip, build, 0)
+
+    for copy in weight_loads:
+        copy.wait()
+    for copy in gathers:
+        copy.wait_recv()
+    own_load.wait()
+    features[...] = jnp.transpose(pieces[...].reshape(width, vert_count))
+
+    def mix(lhs, source, before, weight):
+        spread = jnp.dot(lhs, source, preferred_element_type=jnp.float32)
+        mixed = jnp.dot(
+            spread.astype(jnp.bfloat16), weight, preferred_element_type=jnp.float32
+        )
+        return (before.astype(jnp.float32) + jnp.maximum(mixed, 0.0)).astype(jnp.bfloat16)
+
+    hidden_one[...] = mix(adjacency[...], features[...], features[...], weights[0])
+    own_rows = pl.ds(pl.multiple_of(part * part_rows, part_rows), part_rows)
+    hidden_two[...] = mix(
+        adjacency[own_rows, :], hidden_one[...], hidden_one[own_rows, :], weights[1]
+    ).reshape(snaps, vert_dev, width)
+
+    sends = []
+    for step in range(1, snaps):
+        peer = (own + step) % snaps
+        copy = pltpu.make_async_remote_copy(
+            src_ref=hidden_two.at[peer],
+            dst_ref=vertex_rows.at[own],
+            send_sem=spread_send.at[step],
+            recv_sem=spread_recv.at[step],
+            device_id=(peer // snap_dev, (peer % snap_dev) * parts + part),
+            device_id_type=MESH,
+        )
+        copy.start()
+        sends.append(copy)
+    vertex_rows[own] = hidden_two[own]
+    for copy in sends:
+        copy.wait_recv()
+
+    flat = vertex_rows[...].reshape(snaps * vert_dev, width)
+    group_rows = snaps * SUBLANES
+    groups = vert_dev // SUBLANES
+
+    def split(array):
+        array = array.reshape(snaps, groups, SUBLANES, width)
+        return [array[:, at].reshape(group_rows, width) for at in range(groups)]
+
+    def project(at):
+        return split(jnp.dot(flat, weights[at], preferred_element_type=jnp.float32))
+
+    queries, keys, values = project(2), project(3), project(4)
+    before = split(flat.astype(jnp.float32))
+    lane_head = lax.broadcasted_iota(jnp.int32, (group_rows, width), 1) // head_dim
+    row_at = lax.broadcasted_iota(jnp.int32, (group_rows, group_rows), 0)
+    col_at = lax.broadcasted_iota(jnp.int32, (group_rows, group_rows), 1)
+    visible = (row_at % SUBLANES == col_at % SUBLANES) & (
+        col_at // SUBLANES <= row_at // SUBLANES
+    )
+    factor = head_dim ** (-0.5) * math.log2(math.e)
+    results = []
+    for at in range(groups):
+        key = keys[at].astype(jnp.bfloat16)
+        value = values[at].astype(jnp.bfloat16)
+        query = jnp.concatenate(
+            [
+                jnp.where(lane_head == head, queries[at], 0.0).astype(jnp.bfloat16)
+                for head in range(HEADS)
+            ],
+            axis=0,
+        )
+        scores = lax.dot_general(
+            query, key, (((1,), (1,)), ((), ())), preferred_element_type=jnp.float32
+        )
+        attention = []
+        for head in range(HEADS):
+            score = scores[head * group_rows : (head + 1) * group_rows]
+            score = jnp.where(visible, score, masked_score)
+            lifted = jnp.exp2((score - jnp.max(score, axis=-1, keepdims=True)) * factor)
+            scale = 1.0 / jnp.sum(lifted, axis=-1, keepdims=True)
+            attention.append((lifted * scale).astype(jnp.bfloat16))
+        context_all = jnp.dot(
+            jnp.concatenate(attention, axis=0), value, preferred_element_type=jnp.float32
+        )
+        context = context_all[:group_rows]
+        for head in range(1, HEADS):
+            context = jnp.where(
+                lane_head == head, context_all[head * group_rows : (head + 1) * group_rows], context
+            )
+        result = before[at] + jnp.dot(
+            context.astype(jnp.bfloat16), weights[5], preferred_element_type=jnp.float32
+        )
+        results.append(result.reshape(snaps, 1, SUBLANES, width))
+    evolved = jnp.concatenate(results, axis=1).reshape(n_snap, snap_dev, vert_dev, width)
+
+    low = lax.broadcasted_iota(jnp.int32, (n_snap * vert_dev, LANES), 1) < feat_width
+    for at in range(0, n_feat, 2):
+        lanes = slice(at * feat_width, (at + 2) * feat_width)
+        first = evolved[:, 0, :, lanes].reshape(n_snap * vert_dev, LANES)
+        second = evolved[:, 1, :, lanes].reshape(n_snap * vert_dev, LANES)
+        even = jnp.where(low, first, pltpu.roll(second, feat_width, 1))
+        odd = jnp.where(low, pltpu.roll(first, feat_width, 1), second)
+        outgoing[at] = even.astype(jnp.bfloat16).reshape(n_snap, vert_dev, LANES)
+        outgoing[at + 1] = odd.astype(jnp.bfloat16).reshape(n_snap, vert_dev, LANES)
+
+    returns = []
+    for step in range(1, total):
+        peer = (me + step) % total
+        copy = pltpu.make_async_remote_copy(
+            src_ref=outgoing.at[peer % n_feat, peer // n_feat],
+            dst_ref=returned.at[part, own],
+            send_sem=return_send.at[step],
+            recv_sem=return_recv.at[step],
+            device_id=(peer // n_feat, peer % n_feat),
+            device_id_type=MESH,
+        )
+        copy.start()
+        returns.append(copy)
+    returned[part, own] = outgoing[me_feat, me_snap]
+    for copy in gathers + sends:
+        copy.wait_send()
+    for copy in returns:
+        copy.wait_recv()
+    out_ref[...] = jnp.transpose(returned[...].reshape(vert_count, LANES)).reshape(
+        snap_dev, feat_width, vert_count
+    )
+    for copy in returns:
+        copy.wait_send()
+
+
+def on_device_fused(n_snap, n_feat, *operands):
+    node_features, _, _, _, tile_values, layer_one = operands[:6]
+    snap_dev, vert_count, feat_width = node_features.shape
+    _, slot_total, tile_side, _ = tile_values.shape
+    width = layer_one.shape[0]
+    parts = n_feat // snap_dev
+    snaps = n_snap * snap_dev
+    vert_dev = vert_count // (parts * snaps)
+    total = n_snap * n_feat
+    kept = jnp.bfloat16
+    result = pl.pallas_call(
+        functools.partial(fused_kernel, n_snap, n_feat),
+        out_shape=jax.ShapeDtypeStruct((snap_dev, feat_width, vert_count), kept),
+        in_specs=[pl.BlockSpec(memory_space=pltpu.SMEM)] * 3
+        + [pl.BlockSpec(memory_space=pl.ANY)] * 8,
+        out_specs=pl.BlockSpec(memory_space=pltpu.VMEM),
+        scratch_shapes=[
+            pltpu.VMEM((slot_total, tile_side, tile_side), kept),
+            pltpu.VMEM((6, width, width), kept),
+            pltpu.VMEM((n_feat, feat_width, vert_count), kept),
+            pltpu.VMEM((vert_count, vert_count), kept),
+            pltpu.VMEM((vert_count, width), kept),
+            pltpu.VMEM((vert_count, width), kept),
+            pltpu.VMEM((snaps, vert_dev, width), kept),
+            pltpu.VMEM((snaps, vert_dev, width), kept),
+            pltpu.VMEM((n_feat, n_snap, vert_dev, LANES), kept),
+            pltpu.VMEM((parts, snaps, vert_dev, LANES), kept),
+            pltpu.SemaphoreType.DMA((8,)),
+            pltpu.SemaphoreType.DMA((n_feat,)),
+            pltpu.SemaphoreType.DMA((n_feat,)),
+            pltpu.SemaphoreType.DMA((snaps,)),
+            pltpu.SemaphoreType.DMA((snaps,)),
+            pltpu.SemaphoreType.DMA((total,)),
+            pltpu.SemaphoreType.DMA((total,)),
+        ],
+        compiler_params=pltpu.CompilerParams(collective_id=0, has_side_effects=True),
+    )(*operands[1:4], node_features.transpose(0, 2, 1), *operands[4:])
+    return result.transpose(0, 2, 1)
+
+
+def dispatch(n_snap, n_feat, *operands):
+    snap_dev, vert_count, feat_width = operands[0].shape
+    slot_total = operands[4].shape[1]
+    snaps = n_snap * snap_dev
+    fits = (
+        snap_dev == 2
+        and 2 * feat_width == LANES
+        and n_feat % snap_dev == 0
+        and n_feat % 2 == 0
+        and vert_count % (n_feat // snap_dev * snaps * 2 * SUBLANES) == 0
+        and snaps * SUBLANES == LANES
+        and slot_total <= 16
+        and vert_count <= 1024
+    )
+    if fits:
+        return on_device_fused(n_snap, n_feat, *operands)
+    return on_device(*operands)
+
+
 def solution(mesh):
     placed = (
         P("snap", None, "feat"),
@@ -143,5 +452,5 @@
         P(),
     )
     return jax.shard_map(
-        on_device, mesh=mesh, in_specs=placed, out_specs=P("snap", None, "feat"), check_vma=False
-    )
+        functools.partial(dispatch, mesh.shape["snap"], mesh.shape["feat"]), mesh=mesh, in_specs=placed, out_specs=P("snap", None, "feat"), check_vma=False
+    )

time: 81.8 us -> 28.9 us (0.35)
  blocking collectives: 46 us -> 0 us
  Pallas kernels: 0 us -> 27.2 us
  local copies, waits for them, and re-layouts: 20.4 us -> 1.57 us
  matrix products: 4.96 us -> 0 us
  waiting for transfers between devices: 4.55 us -> 0 us
  starting transfers between devices: 3.33 us -> 0 us
  other arithmetic: 1.48 us -> 0 us
    all_to_all x3 -> x0, blocking collectives: 29.9 us -> none  [the longest x1 13.1 us: on_device(): lax.all_to_all(hidden_two, 'snap', split_axis=1, concat_axis=0, tiled=True)]
    pallas_call x0 -> x1, Pallas kernels: none -> 27.2 us  [on_device_fused(): pl.pallas_call(functools.partial(fused_kernel, n_snap, n_feat), out_shape...]
    all_gather x2 -> x0, blocking collectives: 16.1 us -> none  [convolve(): lax.all_gather(spread_rows, 'feat', axis=1, tiled=True)]
    unnamed x30 -> x1, local copies, waits for them, and re-layouts: 8.75 us -> 1.57 us
    all_to_all x1 -> x0, waiting for transfers between devices: 4.55 us -> none  [on_device(): lax.all_to_all(lax.all_to_all(hidden_two, 'snap', split_axis=1, concat_ax...]
    dot_general x15 -> x0, matrix products: 3.93 us -> none  [the longest x4 1.09 us: spread_padded(): jnp.einsum('irc,icf->irf', tile_block, picked_blocks, preferred_element_t...]
    all_to_all x1 -> x0, starting transfers between devices: 3.33 us -> none  [on_device(): lax.all_to_all(lax.all_to_all(hidden_two, 'snap', split_axis=1, concat_ax...]
    reshape x12 -> x0, local copies, waits for them, and re-layouts: 3.21 us -> none  [the longest x1 0.95 us: attend_local(): return result.astype(jnp.bfloat16).reshape(snaps, verts, model_width)]
  transfers between devices with their start and end apart: 1 -> 0, of which waited for: 1 -> 0; matrix products, arithmetic and copies ran while one was open for 0% -> 0% of each run, Pallas kernels for 0% -> 0%
where the time goes in v1:
time: 28.9 us; the launch traced here: 28.7 us
  Pallas kernels  27.2 us (94%)
  local copies, waits for them, and re-layouts  1.57 us (5%)
    pallas_call x1, Pallas kernels, on_device_fused(): pl.pallas_call(functools.partial(fused_kernel, n_snap, n_feat), out_shape...  27.2 us
    unnamed x1, local copies, waits for them, and re-layouts  1.57 us

profile of v1, /device:TPU:0, one launch (start us, length us, event | category | flops | bytes accessed | tf_op | source)
XLA Modules:
  0.0 28.7 jit_solution(17221083837866024379)
XLA Ops:
  0.0 27.2 %shard_map.109 = bf16[2,64,512]{2,1,0:T(8,128)(2,1)} custom-call(s32[2,8]{1,0:T(2,128)} %rows_ref.1, s32[2,8]{1,0:T(2,128)} %cols_ref.1, s32[2]{0:T(128)} %counts_ref.1, bf16[2,64,512]{2,1,0:T(8,128)(2,1)} %bitcast.3, bf16[2,8,128,128]{3,2,1,0:T(8,128)(2,1)} %tiles_ref.1, bf16[256,256]{1,0:T(8,128)(2,1)} %w_one.1, bf16[256,256]{1,0:T(8,128)(2,1)} %w_two.1, ...), custom_call_target="tpu_custom_call" | custom-call | tf_op jit(solution)/shard_map/pallas_call | solution.py:391
  27.2 1.6 %copy.13 = bf16[2,512,64]{1,2,0:T(8,128)(2,1)} copy(bf16[2,512,64]{1,2,0:T(8,128)(2,1)} %bitcast.2) | data formatting | bytes 262144

commit v2 on v1

--- a/solution.py
+++ b/solution.py
@@ -170,6 +170,7 @@
     spread_recv,
     return_send,
     return_recv,
+    heard,
 ):
     snap_dev, feat_width, vert_count = feat_ref.shape
     slot_total, tile_side, _ = tiles.shape
@@ -199,13 +200,19 @@
     ]
 
     barrier = pltpu.get_barrier_semaphore()
-    for step in range(1, total):
-        peer = (me + step) % total
-        pl.semaphore_signal(
-            barrier, inc=1, device_id=(peer // n_feat, peer % n_feat), device_id_type=MESH
-        )
-
-    pl.semaphore_wait(barrier, total - 1)
+    twin = me_snap + 1 - 2 * (me_snap % 2)
+    ring = [(me_snap + 2) % n_snap, (me_snap + n_snap - 2) % n_snap]
+    mates = [(me_feat + step) % n_feat for step in range(1, n_feat)]
+
+    def tell(semaphore, peers):
+        for peer in peers:
+            pl.semaphore_signal(semaphore, inc=1, device_id=peer, device_id_type=MESH)
+
+    ring_peers = [(peer, me_feat) for peer in ring]
+    twin_peer = [(twin, me_feat)]
+    mate_peers = [(me_snap, mate) for mate in mates]
+    tell(barrier, ring_peers + twin_peer + mate_peers)
+    pl.semaphore_wait(barrier, len(ring_peers) + 1 + len(mate_peers))
 
     gathers = []
     for step in [n_feat // 2] + [s for s in range(1, n_feat) if s != n_feat // 2]:
@@ -221,6 +228,12 @@
         copy.start()
         gathers.append(copy)
     own_load = load(feat_ref.at[local], pieces.at[me_feat], 0)
+
+    hops = n_snap // 4 - 1
+    for hop in range(hops):
+        tell(heard.at[hop], ring_peers)
+        if hop + 1 < hops:
+            pl.semaphore_wait(heard.at[hop], len(ring_peers))
 
     tile_load.wait()
     slot_count = counts_ref[local]
@@ -249,7 +262,13 @@
                 )
         return carry
 
-    lax.fori_loop(0, tile_side // strip, build, 0)
+    strips = tile_side // strip
+    lax.fori_loop(0, strips // 2, build, 0)
+    pl.semaphore_wait(heard.at[hops - 1], len(ring_peers))
+    tell(heard.at[hops], twin_peer)
+    lax.fori_loop(strips // 2, strips, build, 0)
+    pl.semaphore_wait(heard.at[hops], 1)
+    tell(heard.at[hops + 1], mate_peers)
 
     for copy in weight_loads:
         copy.wait()
@@ -271,8 +290,10 @@
         adjacency[own_rows, :], hidden_one[...], hidden_one[own_rows, :], weights[1]
     ).reshape(snaps, vert_dev, width)
 
+    pl.semaphore_wait(heard.at[hops + 1], len(mate_peers))
+
     sends = []
-    for step in range(1, snaps):
+    for step in sorted(range(1, snaps), key=lambda s: abs(2 * s - snaps)):
         peer = (own + step) % snaps
         copy = pltpu.make_async_remote_copy(
             src_ref=hidden_two.at[peer],
@@ -354,7 +375,7 @@
         outgoing[at + 1] = odd.astype(jnp.bfloat16).reshape(n_snap, vert_dev, LANES)
 
     returns = []
-    for step in range(1, total):
+    for step in sorted(range(1, total), key=lambda s: abs(2 * s - total)):
         peer = (me + step) % total
         copy = pltpu.make_async_remote_copy(
             src_ref=outgoing.at[peer % n_feat, peer // n_feat],
@@ -412,6 +433,7 @@
             pltpu.SemaphoreType.DMA((snaps,)),
             pltpu.SemaphoreType.DMA((total,)),
             pltpu.SemaphoreType.DMA((total,)),
+            pltpu.SemaphoreType.REGULAR((n_snap // 4 + 1,)),
         ],
         compiler_params=pltpu.CompilerParams(collective_id=0, has_side_effects=True),
     )(*operands[1:4], node_features.transpose(0, 2, 1), *operands[4:])
@@ -427,6 +449,8 @@
         and 2 * feat_width == LANES
         and n_feat % snap_dev == 0
         and n_feat % 2 == 0
+        and n_snap >= 8
+        and n_snap % 4 == 0
         and vert_count % (n_feat // snap_dev * snaps * 2 * SUBLANES) == 0
         and snaps * SUBLANES == LANES
         and slot_total <= 16

time: 28.9 us -> 28.4 us (0.983)
  Pallas kernels: 27.2 us -> 26.7 us
    pallas_call x1, Pallas kernels: 27.2 us -> 26.7 us  [on_device_fused(): pl.pallas_call(functools.partial(fused_kernel, n_snap, n_feat), out_shape...]
where the time goes in v2:
time: 28.4 us; the launch traced here: 28.3 us
  Pallas kernels  26.7 us (94%)
  local copies, waits for them, and re-layouts  1.57 us (6%)
    pallas_call x1, Pallas kernels, on_device_fused(): pl.pallas_call(functools.partial(fused_kernel, n_snap, n_feat), out_shape...  26.7 us
    unnamed x1, local copies, waits for them, and re-layouts  1.57 us

profile of v2, /device:TPU:0, one launch (start us, length us, event | category | flops | bytes accessed | tf_op | source)
XLA Modules:
  0.0 28.3 jit_solution(8188386899556127901)
XLA Ops:
  0.0 26.7 %shard_map.109 = bf16[2,64,512]{2,1,0:T(8,128)(2,1)} custom-call(s32[2,8]{1,0:T(2,128)} %rows_ref.1, s32[2,8]{1,0:T(2,128)} %cols_ref.1, s32[2]{0:T(128)} %counts_ref.1, bf16[2,64,512]{2,1,0:T(8,128)(2,1)} %bitcast.3, bf16[2,8,128,128]{3,2,1,0:T(8,128)(2,1)} %tiles_ref.1, bf16[256,256]{1,0:T(8,128)(2,1)} %w_one.1, bf16[256,256]{1,0:T(8,128)(2,1)} %w_two.1, ...), custom_call_target="tpu_custom_call" | custom-call | tf_op jit(solution)/shard_map/pallas_call | solution.py:412
  26.7 1.6 %copy.13 = bf16[2,512,64]{1,2,0:T(8,128)(2,1)} copy(bf16[2,512,64]{1,2,0:T(8,128)(2,1)} %bitcast.2) | data formatting | bytes 262144

commit v3 on v2

--- a/solution.py
+++ b/solution.py
@@ -141,9 +141,9 @@
 def fused_kernel(
     n_snap,
     n_feat,
-    rows_ref,
-    cols_ref,
-    counts_ref,
+    rows_hbm,
+    cols_hbm,
+    counts_hbm,
     feat_ref,
     tiles_ref,
     w_one,
@@ -152,7 +152,7 @@
     w_key,
     w_value,
     w_out,
-    out_ref,
+    returned,
     tiles,
     weights,
     pieces,
@@ -162,7 +162,6 @@
     hidden_two,
     vertex_rows,
     outgoing,
-    returned,
     load_sem,
     gather_send,
     gather_recv,
@@ -171,6 +170,9 @@
     return_send,
     return_recv,
     heard,
+    rows_ref,
+    cols_ref,
+    counts_ref,
 ):
     snap_dev, feat_width, vert_count = feat_ref.shape
     slot_total, tile_side, _ = tiles.shape
@@ -193,6 +195,12 @@
         copy.start()
         return copy
 
+    list_loads = [
+        load(ref, kept, 8 + at)
+        for at, (ref, kept) in enumerate(
+            ((rows_hbm, rows_ref), (cols_hbm, cols_ref), (counts_hbm, counts_ref))
+        )
+    ]
     tile_load = load(tiles_ref.at[local], tiles, 1)
     weight_loads = [
         load(ref, weights.at[at], 2 + at)
@@ -236,6 +244,8 @@
             pl.semaphore_wait(heard.at[hop], len(ring_peers))
 
     tile_load.wait()
+    for copy in list_loads:
+        copy.wait()
     slot_count = counts_ref[local]
     strip = 2 * SUBLANES
     places = []
@@ -387,14 +397,12 @@
         )
         copy.start()
         returns.append(copy)
-    returned[part, own] = outgoing[me_feat, me_snap]
+    own_copy = load(outgoing.at[me_feat, me_snap], returned.at[part, own], 0)
     for copy in gathers + sends:
         copy.wait_send()
+    own_copy.wait()
     for copy in returns:
         copy.wait_recv()
-    out_ref[...] = jnp.transpose(returned[...].reshape(vert_count, LANES)).reshape(
-        snap_dev, feat_width, vert_count
-    )
     for copy in returns:
         copy.wait_send()
 
@@ -411,10 +419,9 @@
     kept = jnp.bfloat16
     result = pl.pallas_call(
         functools.partial(fused_kernel, n_snap, n_feat),
-        out_shape=jax.ShapeDtypeStruct((snap_dev, feat_width, vert_count), kept),
-        in_specs=[pl.BlockSpec(memory_space=pltpu.SMEM)] * 3
-        + [pl.BlockSpec(memory_space=pl.ANY)] * 8,
-        out_specs=pl.BlockSpec(memory_space=pltpu.VMEM),
+        out_shape=jax.ShapeDtypeStruct((parts, snaps, vert_dev, LANES), kept),
+        in_specs=[pl.BlockSpec(memory_space=pltpu.HBM)] * 11,
+        out_specs=pl.BlockSpec(memory_space=pl.ANY),
         scratch_shapes=[
             pltpu.VMEM((slot_total, tile_side, tile_side), kept),
             pltpu.VMEM((6, width, width), kept),
@@ -425,8 +432,7 @@
             pltpu.VMEM((snaps, vert_dev, width), kept),
             pltpu.VMEM((snaps, vert_dev, width), kept),
             pltpu.VMEM((n_feat, n_snap, vert_dev, LANES), kept),
-            pltpu.VMEM((parts, snaps, vert_dev, LANES), kept),
-            pltpu.SemaphoreType.DMA((8,)),
+            pltpu.SemaphoreType.DMA((11,)),
             pltpu.SemaphoreType.DMA((n_feat,)),
             pltpu.SemaphoreType.DMA((n_feat,)),
             pltpu.SemaphoreType.DMA((snaps,)),
@@ -434,10 +440,14 @@
             pltpu.SemaphoreType.DMA((total,)),
             pltpu.SemaphoreType.DMA((total,)),
             pltpu.SemaphoreType.REGULAR((n_snap // 4 + 1,)),
+            pltpu.SMEM((snap_dev, slot_total), jnp.int32),
+            pltpu.SMEM((snap_dev, slot_total), jnp.int32),
+            pltpu.SMEM((snap_dev,), jnp.int32),
         ],
-        compiler_params=pltpu.CompilerParams(collective_id=0, has_side_effects=True),
+        compiler_params=pltpu.CompilerParams(collective_id=0, has_side_effects=True, vmem_limit_bytes=8388608),
     )(*operands[1:4], node_features.transpose(0, 2, 1), *operands[4:])
-    return result.transpose(0, 2, 1)
+    result = jnp.transpose(result.reshape(vert_count, LANES))
+    return result.reshape(snap_dev, feat_width, vert_count).transpose(0, 2, 1)
 
 
 def dispatch(n_snap, n_feat, *operands):

time: 28.4 us -> 35.9 us (1.26)
  local copies, waits for them, and re-layouts: 1.57 us -> 9.51 us
  Pallas kernels: 26.7 us -> 26.1 us
    unnamed x1 -> x22, local copies, waits for them, and re-layouts: 1.57 us -> 8.74 us
    transpose x0 -> x1, local copies, waits for them, and re-layouts: none -> 0.77 us  [on_device_fused(): result = jnp.transpose(result.reshape(vert_count, LANES))]
    pallas_call x1, Pallas kernels: 26.7 us -> 26.1 us  [on_device_fused(): pl.pallas_call(functools.partial(fused_kernel, n_snap, n_feat), out_shape...]
where the time goes in v3:
time: 35.9 us; the launch traced here: 35.6 us
  Pallas kernels  26.1 us (73%)
  local copies, waits for them, and re-layouts  9.51 us (26%)
    pallas_call x1, Pallas kernels, on_device_fused(): pl.pallas_call(functools.partial(fused_kernel, n_snap, n_feat), out_shape...  26.1 us
    unnamed x22, local copies, waits for them, and re-layouts  8.74 us
    transpose x1, local copies, waits for them, and re-layouts, on_device_fused(): result = jnp.transpose(result.reshape(vert_count, LANES))  0.77 us

profile of v3, /device:TPU:0, one launch (start us, length us, event | category | flops | bytes accessed | tf_op | source)
XLA Modules:
  0.0 35.6 jit_solution(8889156035746049208)
XLA Ops:
  0.0 0.0 copy-start.10
  0.0 0.0 copy-start.8
  0.0 0.7 %copy-done.10 = s32[2]{0:T(128)S(1)} copy-done((s32[2]{0:T(128)S(1)}, s32[2]{0:T(128)}, u32[]{:S(2)}) %copy-start.10) | copy-done | bytes 32
  0.7 0.0 copy-done.8
  0.7 0.0 copy-start
  0.7 1.0 %copy-done = bf16[2,8,128,128]{3,2,1,0:T(8,128)(2,1)S(1)} copy-done((bf16[2,8,128,128]{3,2,1,0:T(8,128)(2,1)S(1)}, bf16[2,8,128,128]{3,2,1,0:T(8,128)(2,1)}, u32[]{:S(2)}) %copy-start) | copy-done | bytes 524312
  1.7 0.0 copy-start.1
  1.7 0.9 %copy-done.1 = bf16[2,512,64]{1,2,0:T(8,128)(2,1)S(1)} copy-done((bf16[2,512,64]{1,2,0:T(8,128)(2,1)S(1)}, bf16[2,512,64]{1,2,0:T(8,128)(2,1)}, u32[]{:S(2)}) %copy-start.1) | copy-done | bytes 131096
  2.6 0.0 copy-start.2
  2.6 0.9 %copy-done.2 = bf16[256,256]{1,0:T(8,128)(2,1)S(1)} copy-done((bf16[256,256]{1,0:T(8,128)(2,1)S(1)}, bf16[256,256]{1,0:T(8,128)(2,1)}, u32[]{:S(2)}) %copy-start.2) | copy-done | bytes 131096
  3.5 0.0 copy-start.3
  3.5 0.9 %copy-done.3 = bf16[256,256]{1,0:T(8,128)(2,1)S(1)} copy-done((bf16[256,256]{1,0:T(8,128)(2,1)S(1)}, bf16[256,256]{1,0:T(8,128)(2,1)}, u32[]{:S(2)}) %copy-start.3) | copy-done | bytes 131096
  4.5 0.0 copy-start.4
  4.5 0.9 %copy-done.4 = bf16[256,256]{1,0:T(8,128)(2,1)S(1)} copy-done((bf16[256,256]{1,0:T(8,128)(2,1)S(1)}, bf16[256,256]{1,0:T(8,128)(2,1)}, u32[]{:S(2)}) %copy-start.4) | copy-done | bytes 131096
  5.4 0.0 copy-start.5
  5.4 0.9 %copy-done.5 = bf16[256,256]{1,0:T(8,128)(2,1)S(1)} copy-done((bf16[256,256]{1,0:T(8,128)(2,1)S(1)}, bf16[256,256]{1,0:T(8,128)(2,1)}, u32[]{:S(2)}) %copy-start.5) | copy-done | bytes 131096
  6.3 0.0 copy-start.6
  6.3 0.9 %copy-done.6 = bf16[256,256]{1,0:T(8,128)(2,1)S(1)} copy-done((bf16[256,256]{1,0:T(8,128)(2,1)S(1)}, bf16[256,256]{1,0:T(8,128)(2,1)}, u32[]{:S(2)}) %copy-start.6) | copy-done | bytes 131096
  7.2 0.0 copy-start.7
  7.2 0.9 %copy-done.7 = bf16[256,256]{1,0:T(8,128)(2,1)S(1)} copy-done((bf16[256,256]{1,0:T(8,128)(2,1)S(1)}, bf16[256,256]{1,0:T(8,128)(2,1)}, u32[]{:S(2)}) %copy-start.7) | copy-done | bytes 131096
  8.1 0.0 copy-start.9
  8.1 0.7 %copy-done.9 = s32[2,8]{1,0:T(2,128)S(1)} copy-done((s32[2,8]{1,0:T(2,128)S(1)}, s32[2,8]{1,0:T(2,128)}, u32[]{:S(2)}) %copy-start.9) | copy-done | bytes 88
  8.8 26.1 %shard_map.109 = bf16[2,16,16,128]{3,2,1,0:T(8,128)(2,1)S(1)} custom-call(s32[2,8]{1,0:T(2,128)S(1)} %copy-done.8, s32[2,8]{1,0:T(2,128)S(1)} %copy-done.9, s32[2]{0:T(128)S(1)} %copy-done.10, bf16[2,64,512]{2,1,0:T(8,128)(2,1)S(1)} %bitcast.8, bf16[2,8,128,128]{3,2,1,0:T(8,128)(2,1)S(1)} %copy-done, bf16[256,256]{1,0:T(8,128)(2,1)S(1)} %copy-done.2, ...), custom_call_target="tpu_custom_call" | custom-call | tf_op jit(solution)/shard_map/pallas_call | solution.py:420
  34.9 0.8 %copy.12 = bf16[128,512]{1,0:T(8,128)(2,1)} copy(bf16[128,512]{0,1:T(8,128)(2,1)S(1)} %bitcast.7) | data formatting | bytes 262144 | tf_op jit(solution)/shard_map/transpose | solution.py:449
Async XLA Ops:
  0.0 0.7 %copy-start.10 = (s32[2]{0:T(128)S(1)}, s32[2]{0:T(128)}, u32[]{:S(2)}) copy-start(s32[2]{0:T(128)} %counts_hbm.1) | copy-start | bytes 28
  0.0 0.7 %copy-start.8 = (s32[2,8]{1,0:T(2,128)S(1)}, s32[2,8]{1,0:T(2,128)}, u32[]{:S(2)}) copy-start(s32[2,8]{1,0:T(2,128)} %rows_hbm.1) | copy-start | bytes 196
  0.7 1.0 %copy-start = (bf16[2,8,128,128]{3,2,1,0:T(8,128)(2,1)S(1)}, bf16[2,8,128,128]{3,2,1,0:T(8,128)(2,1)}, u32[]{:S(2)}) copy-start(bf16[2,8,128,128]{3,2,1,0:T(8,128)(2,1)} %tiles_ref.1) | copy-start | bytes 1572868
  1.7 0.9 %copy-start.1 = (bf16[2,512,64]{1,2,0:T(8,128)(2,1)S(1)}, bf16[2,512,64]{1,2,0:T(8,128)(2,1)}, u32[]{:S(2)}) copy-start(bf16[2,512,64]{1,2,0:T(8,128)(2,1)} %param.11) | copy-start | bytes 393220
  2.6 0.9 %copy-start.2 = (bf16[256,256]{1,0:T(8,128)(2,1)S(1)}, bf16[256,256]{1,0:T(8,128)(2,1)}, u32[]{:S(2)}) copy-start(bf16[256,256]{1,0:T(8,128)(2,1)} %w_one.1) | copy-start | bytes 393220
  3.5 0.9 %copy-start.3 = (bf16[256,256]{1,0:T(8,128)(2,1)S(1)}, bf16[256,256]{1,0:T(8,128)(2,1)}, u32[]{:S(2)}) copy-start(bf16[256,256]{1,0:T(8,128)(2,1)} %w_two.1) | copy-start | bytes 393220
  4.5 0.9 %copy-start.4 = (bf16[256,256]{1,0:T(8,128)(2,1)S(1)}, bf16[256,256]{1,0:T(8,128)(2,1)}, u32[]{:S(2)}) copy-start(bf16[256,256]{1,0:T(8,128)(2,1)} %w_query.1) | copy-start | bytes 393220
  5.4 0.9 %copy-start.5 = (bf16[256,256]{1,0:T(8,128)(2,1)S(1)}, bf16[256,256]{1,0:T(8,128)(2,1)}, u32[]{:S(2)}) copy-start(bf16[256,256]{1,0:T(8,128)(2,1)} %w_key.1) | copy-start | bytes 393220
  6.3 0.9 %copy-start.6 = (bf16[256,256]{1,0:T(8,128)(2,1)S(1)}, bf16[256,256]{1,0:T(8,128)(2,1)}, u32[]{:S(2)}) copy-start(bf16[256,256]{1,0:T(8,128)(2,1)} %w_value.1) | copy-start | bytes 393220
  7.2 0.9 %copy-start.7 = (bf16[256,256]{1,0:T(8,128)(2,1)S(1)}, bf16[256,256]{1,0:T(8,128)(2,1)}, u32[]{:S(2)}) copy-start(bf16[256,256]{1,0:T(8,128)(2,1)} %w_out.1) | copy-start | bytes 393220
  8.1 0.7 %copy-start.9 = (s32[2,8]{1,0:T(2,128)S(1)}, s32[2,8]{1,0:T(2,128)}, u32[]{:S(2)}) copy-start(s32[2,8]{1,0:T(2,128)} %cols_hbm.1) | copy-start | bytes 196

commit v4 on v3

--- a/solution.py
+++ b/solution.py
@@ -444,7 +444,7 @@
             pltpu.SMEM((snap_dev, slot_total), jnp.int32),
             pltpu.SMEM((snap_dev,), jnp.int32),
         ],
-        compiler_params=pltpu.CompilerParams(collective_id=0, has_side_effects=True, vmem_limit_bytes=8388608),
+        compiler_params=pltpu.CompilerParams(collective_id=0, has_side_effects=True),
     )(*operands[1:4], node_features.transpose(0, 2, 1), *operands[4:])
     result = jnp.transpose(result.reshape(vert_count, LANES))
     return result.reshape(snap_dev, feat_width, vert_count).transpose(0, 2, 1)

time: 35.9 us -> 27.2 us (0.76)
  local copies, waits for them, and re-layouts: 9.51 us -> 1.67 us
  Pallas kernels: 26.1 us -> 25.4 us
    unnamed x22 -> x0, local copies, waits for them, and re-layouts: 8.74 us -> none
    transpose x1, local copies, waits for them, and re-layouts: 0.77 us -> 1.67 us  [on_device_fused(): result = jnp.transpose(result.reshape(vert_count, LANES))]
    pallas_call x1, Pallas kernels: 26.1 us -> 25.4 us  [on_device_fused(): pl.pallas_call(functools.partial(fused_kernel, n_snap, n_feat), out_shape...]
where the time goes in v4:
time: 27.2 us; the launch traced here: 27 us
  Pallas kernels  25.4 us (93%)
  local copies, waits for them, and re-layouts  1.67 us (6%)
    pallas_call x1, Pallas kernels, on_device_fused(): pl.pallas_call(functools.partial(fused_kernel, n_snap, n_feat), out_shape...  25.4 us
    transpose x1, local copies, waits for them, and re-layouts, on_device_fused(): result = jnp.transpose(result.reshape(vert_count, LANES))  1.67 us

profile of v4, /device:TPU:0, one launch (start us, length us, event | category | flops | bytes accessed | tf_op | source)
XLA Modules:
  0.0 27.0 jit_solution(10539621370344439553)
XLA Ops:
  0.0 25.4 %shard_map.109 = bf16[2,16,16,128]{3,2,1,0:T(8,128)(2,1)} custom-call(s32[2,8]{1,0:T(2,128)} %rows_hbm.1, s32[2,8]{1,0:T(2,128)} %cols_hbm.1, s32[2]{0:T(128)} %counts_hbm.1, bf16[2,64,512]{2,1,0:T(8,128)(2,1)} %bitcast.8, bf16[2,8,128,128]{3,2,1,0:T(8,128)(2,1)} %tiles_ref.1, bf16[256,256]{1,0:T(8,128)(2,1)} %w_one.1, bf16[256,256]{1,0:T(8,128)(2,1)} %w_two.1, ...), custom_call_target="tpu_custom_call" | custom-call | tf_op jit(solution)/shard_map/pallas_call | solution.py:420
  25.4 1.7 %copy.12 = bf16[128,512]{1,0:T(8,128)(2,1)} copy(bf16[128,512]{0,1:T(8,128)(2,1)} %bitcast.7) | data formatting | bytes 262144 | tf_op jit(solution)/shard_map/transpose | solution.py:449

commit v5 on v4

--- a/solution.py
+++ b/solution.py
@@ -295,29 +295,35 @@
         return (before.astype(jnp.float32) + jnp.maximum(mixed, 0.0)).astype(jnp.bfloat16)
 
     hidden_one[...] = mix(adjacency[...], features[...], features[...], weights[0])
-    own_rows = pl.ds(pl.multiple_of(part * part_rows, part_rows), part_rows)
-    hidden_two[...] = mix(
-        adjacency[own_rows, :], hidden_one[...], hidden_one[own_rows, :], weights[1]
-    ).reshape(snaps, vert_dev, width)
-
     pl.semaphore_wait(heard.at[hops + 1], len(mate_peers))
-
+    side = snaps // 2
+    side_rows = side * vert_dev
     sends = []
-    for step in sorted(range(1, snaps), key=lambda s: abs(2 * s - snaps)):
-        peer = (own + step) % snaps
-        copy = pltpu.make_async_remote_copy(
-            src_ref=hidden_two.at[peer],
-            dst_ref=vertex_rows.at[own],
-            send_sem=spread_send.at[step],
-            recv_sem=spread_recv.at[step],
-            device_id=(peer // snap_dev, (peer % snap_dev) * parts + part),
-            device_id_type=MESH,
-        )
-        copy.start()
-        sends.append(copy)
+    for turn in range(2):
+        first = (own // side + 1 - turn) % 2 * side
+        start = pl.multiple_of(part * part_rows + first * vert_dev, side_rows)
+        own_rows = pl.ds(start, side_rows)
+        hidden_two[pl.ds(first, side)] = mix(
+            adjacency[own_rows, :], hidden_one[...], hidden_one[own_rows, :], weights[1]
+        ).reshape(side, vert_dev, width)
+        for step in range(turn, side):
+            peer = first + (own % side + step) % side
+            at = step + (1 - turn) * side
+            copy = pltpu.make_async_remote_copy(
+                src_ref=hidden_two.at[peer],
+                dst_ref=vertex_rows.at[own],
+                send_sem=spread_send.at[at],
+                recv_sem=spread_recv.at[(own - peer + snaps) % snaps],
+                device_id=(peer // snap_dev, (peer % snap_dev) * parts + part),
+                device_id_type=MESH,
+            )
+            copy.start()
+            sends.append(copy)
     vertex_rows[own] = hidden_two[own]
-    for copy in sends:
-        copy.wait_recv()
+    for source in range(1, snaps):
+        pltpu.make_async_copy(
+            hidden_two.at[0], vertex_rows.at[0], spread_recv.at[source]
+        ).wait()
 
     flat = vertex_rows[...].reshape(snaps * vert_dev, width)
     group_rows = snaps * SUBLANES
@@ -336,41 +342,38 @@
     row_at = lax.broadcasted_iota(jnp.int32, (group_rows, group_rows), 0)
     col_at = lax.broadcasted_iota(jnp.int32, (group_rows, group_rows), 1)
     visible = (row_at % SUBLANES == col_at % SUBLANES) & (
-        col_at // SUBLANES <= row_at // SUBLANES
+        row_at // SUBLANES <= col_at // SUBLANES
     )
     factor = head_dim ** (-0.5) * math.log2(math.e)
     results = []
     for at in range(groups):
-        key = keys[at].astype(jnp.bfloat16)
-        value = values[at].astype(jnp.bfloat16)
-        query = jnp.concatenate(
+        query = queries[at].astype(jnp.bfloat16)
+        value = jnp.transpose(values[at].astype(jnp.bfloat16))
+        key = jnp.concatenate(
             [
-                jnp.where(lane_head == head, queries[at], 0.0).astype(jnp.bfloat16)
+                jnp.where(lane_head == head, keys[at], 0.0).astype(jnp.bfloat16)
                 for head in range(HEADS)
             ],
             axis=0,
         )
         scores = lax.dot_general(
-            query, key, (((1,), (1,)), ((), ())), preferred_element_type=jnp.float32
-        )
-        attention = []
+            key, query, (((1,), (1,)), ((), ())), preferred_element_type=jnp.float32
+        )
+        context = []
         for head in range(HEADS):
             score = scores[head * group_rows : (head + 1) * group_rows]
             score = jnp.where(visible, score, masked_score)
-            lifted = jnp.exp2((score - jnp.max(score, axis=-1, keepdims=True)) * factor)
-            scale = 1.0 / jnp.sum(lifted, axis=-1, keepdims=True)
-            attention.append((lifted * scale).astype(jnp.bfloat16))
-        context_all = jnp.dot(
-            jnp.concatenate(attention, axis=0), value, preferred_element_type=jnp.float32
-        )
-        context = context_all[:group_rows]
-        for head in range(1, HEADS):
-            context = jnp.where(
-                lane_head == head, context_all[head * group_rows : (head + 1) * group_rows], context
+            lifted = jnp.exp2((score - jnp.max(score, axis=0, keepdims=True)) * factor)
+            scale = 1.0 / jnp.sum(lifted, axis=0, keepdims=True)
+            context.append(
+                jnp.dot(
+                    value[head * head_dim : (head + 1) * head_dim],
+                    (lifted * scale).astype(jnp.bfloat16),
+                    preferred_element_type=jnp.float32,
+                )
             )
-        result = before[at] + jnp.dot(
-            context.astype(jnp.bfloat16), weights[5], preferred_element_type=jnp.float32
-        )
+        context = jnp.transpose(jnp.concatenate(context, axis=0).astype(jnp.bfloat16))
+        result = before[at] + jnp.dot(context, weights[5], preferred_element_type=jnp.float32)
         results.append(result.reshape(snaps, 1, SUBLANES, width))
     evolved = jnp.concatenate(results, axis=1).reshape(n_snap, snap_dev, vert_dev, width)
 

time: 27.2 us -> 26.1 us (0.960)
  Pallas kernels: 25.4 us -> 24.3 us
    pallas_call x1, Pallas kernels: 25.4 us -> 24.3 us  [on_device_fused(): pl.pallas_call(functools.partial(fused_kernel, n_snap, n_feat), out_shape...]
where the time goes in v5:
time: 26.1 us; the launch traced here: 26 us
  Pallas kernels  24.3 us (93%)
  local copies, waits for them, and re-layouts  1.67 us (6%)
    pallas_call x1, Pallas kernels, on_device_fused(): pl.pallas_call(functools.partial(fused_kernel, n_snap, n_feat), out_shape...  24.3 us
    transpose x1, local copies, waits for them, and re-layouts, on_device_fused(): result = jnp.transpose(result.reshape(vert_count, LANES))  1.67 us

profile of v5, /device:TPU:0, one launch (start us, length us, event | category | flops | bytes accessed | tf_op | source)
XLA Modules:
  0.0 26.0 jit_solution(2089922628563635197)
XLA Ops:
  0.0 24.3 %shard_map.109 = bf16[2,16,16,128]{3,2,1,0:T(8,128)(2,1)} custom-call(s32[2,8]{1,0:T(2,128)} %rows_hbm.1, s32[2,8]{1,0:T(2,128)} %cols_hbm.1, s32[2]{0:T(128)} %counts_hbm.1, bf16[2,64,512]{2,1,0:T(8,128)(2,1)} %bitcast.8, bf16[2,8,128,128]{3,2,1,0:T(8,128)(2,1)} %tiles_ref.1, bf16[256,256]{1,0:T(8,128)(2,1)} %w_one.1, bf16[256,256]{1,0:T(8,128)(2,1)} %w_two.1, ...), custom_call_target="tpu_custom_call" | custom-call | tf_op jit(solution)/shard_map/pallas_call | solution.py:423
  24.3 1.7 %copy.12 = bf16[128,512]{1,0:T(8,128)(2,1)} copy(bf16[128,512]{0,1:T(8,128)(2,1)} %bitcast.7) | data formatting | bytes 262144 | tf_op jit(solution)/shard_map/transpose | solution.py:452

commit v6 on v5

--- a/solution.py
+++ b/solution.py
@@ -345,7 +345,9 @@
         row_at // SUBLANES <= col_at // SUBLANES
     )
     factor = head_dim ** (-0.5) * math.log2(math.e)
-    results = []
+    low = lax.broadcasted_iota(jnp.int32, (n_snap * SUBLANES, LANES), 1) < feat_width
+    returns = []
+    own_copies = []
     for at in range(groups):
         query = queries[at].astype(jnp.bfloat16)
         value = jnp.transpose(values[at].astype(jnp.bfloat16))
@@ -374,36 +376,36 @@
             )
         context = jnp.transpose(jnp.concatenate(context, axis=0).astype(jnp.bfloat16))
         result = before[at] + jnp.dot(context, weights[5], preferred_element_type=jnp.float32)
-        results.append(result.reshape(snaps, 1, SUBLANES, width))
-    evolved = jnp.concatenate(results, axis=1).reshape(n_snap, snap_dev, vert_dev, width)
-
-    low = lax.broadcasted_iota(jnp.int32, (n_snap * vert_dev, LANES), 1) < feat_width
-    for at in range(0, n_feat, 2):
-        lanes = slice(at * feat_width, (at + 2) * feat_width)
-        first = evolved[:, 0, :, lanes].reshape(n_snap * vert_dev, LANES)
-        second = evolved[:, 1, :, lanes].reshape(n_snap * vert_dev, LANES)
-        even = jnp.where(low, first, pltpu.roll(second, feat_width, 1))
-        odd = jnp.where(low, pltpu.roll(first, feat_width, 1), second)
-        outgoing[at] = even.astype(jnp.bfloat16).reshape(n_snap, vert_dev, LANES)
-        outgoing[at + 1] = odd.astype(jnp.bfloat16).reshape(n_snap, vert_dev, LANES)
-
-    returns = []
-    for step in sorted(range(1, total), key=lambda s: abs(2 * s - total)):
-        peer = (me + step) % total
-        copy = pltpu.make_async_remote_copy(
-            src_ref=outgoing.at[peer % n_feat, peer // n_feat],
-            dst_ref=returned.at[part, own],
-            send_sem=return_send.at[step],
-            recv_sem=return_recv.at[step],
-            device_id=(peer // n_feat, peer % n_feat),
-            device_id_type=MESH,
-        )
-        copy.start()
-        returns.append(copy)
-    own_copy = load(outgoing.at[me_feat, me_snap], returned.at[part, own], 0)
+        evolved = result.reshape(n_snap, snap_dev, SUBLANES, width)
+        for pair in range(0, n_feat, 2):
+            lanes = slice(pair * feat_width, (pair + 2) * feat_width)
+            early = evolved[:, 0, :, lanes].reshape(n_snap * SUBLANES, LANES)
+            late = evolved[:, 1, :, lanes].reshape(n_snap * SUBLANES, LANES)
+            even = jnp.where(low, early, pltpu.roll(late, feat_width, 1))
+            odd = jnp.where(low, pltpu.roll(early, feat_width, 1), late)
+            for other, lane_pair in ((pair, even), (pair + 1, odd)):
+                outgoing[other, at] = lane_pair.astype(jnp.bfloat16).reshape(
+                    n_snap, SUBLANES, LANES
+                )
+        for step in sorted(range(1, total), key=lambda s: abs(2 * s - total)):
+            peer = (me + step) % total
+            copy = pltpu.make_async_remote_copy(
+                src_ref=outgoing.at[peer % n_feat, at, peer // n_feat],
+                dst_ref=returned.at[part, own, at],
+                send_sem=return_send.at[at, step],
+                recv_sem=return_recv.at[at, step],
+                device_id=(peer // n_feat, peer % n_feat),
+                device_id_type=MESH,
+            )
+            copy.start()
+            returns.append(copy)
+        own_copies.append(
+            load(outgoing.at[me_feat, at, me_snap], returned.at[part, own, at], at)
+        )
     for copy in gathers + sends:
         copy.wait_send()
-    own_copy.wait()
+    for copy in own_copies:
+        copy.wait()
     for copy in returns:
         copy.wait_recv()
     for copy in returns:
@@ -422,7 +424,7 @@
     kept = jnp.bfloat16
     result = pl.pallas_call(
         functools.partial(fused_kernel, n_snap, n_feat),
-        out_shape=jax.ShapeDtypeStruct((parts, snaps, vert_dev, LANES), kept),
+        out_shape=jax.ShapeDtypeStruct((parts, snaps, vert_dev // SUBLANES, SUBLANES, LANES), kept),
         in_specs=[pl.BlockSpec(memory_space=pltpu.HBM)] * 11,
         out_specs=pl.BlockSpec(memory_space=pl.ANY),
         scratch_shapes=[
@@ -434,14 +436,14 @@
             pltpu.VMEM((vert_count, width), kept),
             pltpu.VMEM((snaps, vert_dev, width), kept),
             pltpu.VMEM((snaps, vert_dev, width), kept),
-            pltpu.VMEM((n_feat, n_snap, vert_dev, LANES), kept),
+            pltpu.VMEM((n_feat, vert_dev // SUBLANES, n_snap, SUBLANES, LANES), kept),
             pltpu.SemaphoreType.DMA((11,)),
             pltpu.SemaphoreType.DMA((n_feat,)),
             pltpu.SemaphoreType.DMA((n_feat,)),
             pltpu.SemaphoreType.DMA((snaps,)),
             pltpu.SemaphoreType.DMA((snaps,)),
-            pltpu.SemaphoreType.DMA((total,)),
-            pltpu.SemaphoreType.DMA((total,)),
+            pltpu.SemaphoreType.DMA((vert_dev // SUBLANES, total)),
+            pltpu.SemaphoreType.DMA((vert_dev // SUBLANES, total)),
             pltpu.SemaphoreType.REGULAR((n_snap // 4 + 1,)),
             pltpu.SMEM((snap_dev, slot_total), jnp.int32),
             pltpu.SMEM((snap_dev, slot_total), jnp.int32),

time: 26.1 us -> 26.4 us (1.011)
  no operation moved by 1% of the time
where the time goes in v6:
time: 26.4 us; the launch traced here: 26.2 us
  Pallas kernels  24.5 us (93%)
  local copies, waits for them, and re-layouts  1.67 us (6%)
    pallas_call x1, Pallas kernels, on_device_fused(): pl.pallas_call(functools.partial(fused_kernel, n_snap, n_feat), out_shape...  24.5 us
    transpose x1, local copies, waits for them, and re-layouts, on_device_fused(): result = jnp.transpose(result.reshape(vert_count, LANES))  1.67 us

profile of v6, /device:TPU:0, one launch (start us, length us, event | category | flops | bytes accessed | tf_op | source)
XLA Modules:
  0.0 26.2 jit_solution(11783313405942862692)
XLA Ops:
  0.0 24.5 %shard_map.109 = bf16[2,16,2,8,128]{4,3,2,1,0:T(8,128)(2,1)} custom-call(s32[2,8]{1,0:T(2,128)} %rows_hbm.1, s32[2,8]{1,0:T(2,128)} %cols_hbm.1, s32[2]{0:T(128)} %counts_hbm.1, bf16[2,64,512]{2,1,0:T(8,128)(2,1)} %bitcast.8, bf16[2,8,128,128]{3,2,1,0:T(8,128)(2,1)} %tiles_ref.1, bf16[256,256]{1,0:T(8,128)(2,1)} %w_one.1, bf16[256,256]{1,0:T(8,128)(2,1)} %w_two.1, ...), custom_call_target="tpu_custom_call" | custom-call | tf_op jit(solution)/shard_map/pallas_call | solution.py:425
  24.5 1.7 %copy.12 = bf16[128,512]{1,0:T(8,128)(2,1)} copy(bf16[128,512]{0,1:T(8,128)(2,1)} %bitcast.7) | data formatting | bytes 262144 | tf_op jit(solution)/shard_map/transpose | solution.py:454
